TPU v7x, 256 devices: a whole 4x4x8 slice. The times are simulated.
256 devices in a mesh: sec: 2 (over x_lo), slab: 64 (over z, y, core), ch: 2 (over x_hi).
Axes of the slice: x: 4 (x_hi: 2, x_lo: 2; x = x_hi * 2 + x_lo), y: 4, z: 8, core: 2. Of those that a mesh axis runs over, the one named last changes fastest.
Arguments:
- latents: bfloat16 [4, 64, 64, 16], P('sec', None, 'slab'), may hold values from -6 to 6
- weight_in: bfloat16 [3, 3, 3, 16, 384], replicated, may hold values from -0.3125 to 0.3125
- weight_mid: bfloat16 [3, 3, 3, 384, 384], replicated, may hold values from -0.0625 to 0.0625
- weight_up: bfloat16 [3, 3, 3, 384, 192], replicated, may hold values from -0.0625 to 0.0625
- reward_grad: bfloat16 [4, 128, 128, 192], P('sec', 'slab', None, 'ch'), may hold values from -6 to 6
Outputs:
- decoded: bfloat16 [4, 128, 128, 192], P('sec', 'slab', None, 'ch')
- latent_grad: float32 [4, 64, 64, 16], P('sec', None, 'slab')
All inputs are finite; a program needn't handle non-finite values.
Results may differ from a plain program's by a relative error of at most 0.0052.
Values may be sent and summed in bfloat16 or wider, within the bound.
A program may use at most 128 MiB of HBM per device.

v0:
```python
import functools

import jax
import jax.numpy as jnp
from jax import lax
from jax.experimental import pallas as pl
from jax.experimental.pallas import tpu as pltpu
from jax.sharding import PartitionSpec as P

EPSILON = 1e-06
MESH = pl.DeviceIdType.MESH
BF = jnp.bfloat16
F32 = jnp.float32
NT = (((1,), (1,)), ((), ()))


def shift_rows(x, step, col, width):
    rolled = pltpu.roll(x, step % x.shape[0], axis=0)
    if step > 0:
        return jnp.where(col < step, 0.0, rolled)
    return jnp.where(col >= width + step, 0.0, rolled)


def kernel(n, lat_in, rew_in, win_hbm, wm_hbm, wu_hbm, dec_out, lg_out,
           wm, wu, win, w1, wz, par, gb, view, lat, lx, xc, h2, g2, sc, seg, n1, s1, n2, s2, acc, zs, zr, up, inter,
           wsem, xs_s, xs_r, rs_s, rs_r, la_s, la_r, hs_s, hs_r, gs_s, gs_r, zsem):
    s = lax.axis_index("sec")
    l = lax.axis_index("slab")
    c = lax.axis_index("ch")
    nxt = lax.rem(l + 1, n)
    prv = lax.rem(l + n - 1, n)
    rows = 4 * n
    c1 = wm.shape[3]

    copies = [
        pltpu.make_async_copy(win_hbm, win, wsem.at[0]),
        pltpu.make_async_copy(wm_hbm, wm, wsem.at[1]),
        pltpu.make_async_copy(wu_hbm, wu, wsem.at[2]),
    ]
    for copy in copies:
        copy.start()

    def remote(src, dst, ss, rs, dev):
        return pltpu.make_async_remote_copy(src_ref=src, dst_ref=dst, send_sem=ss, recv_sem=rs, device_id=dev, device_id_type=MESH)

    lane = lax.broadcasted_iota(jnp.int32, (n, 128), 1)
    row = lax.broadcasted_iota(jnp.int32, (n, 128), 0)
    for f in range(2):
        x = lat_in[f].astype(F32)
        total = jnp.zeros((n, 128), F32)
        for r in range(5):
            moved = shift_rows(x, 2 - r, row, n) if r != 2 else x
            if r:
                moved = pltpu.roll(moved, 16 * r, axis=1)
            total = total + moved
        view[f] = total.reshape(n, 1, 128)

    for i in range(2):
        lat[2 * s + i, l] = view[i, l]
    other = remote(view.at[:, l], lat.at[pl.ds(2 * s, 2), l], la_s.at[1], la_r.at[1], (1 - s, l, c))
    other.start()

    def send_lat(i, carry):
        to = lax.rem(l + i, n)
        remote(view.at[:, to], lat.at[pl.ds(2 * s, 2), l], la_s.at[0], la_r.at[0], (s, to, c)).start()
        remote(view.at[:, to], lat.at[pl.ds(2 * s, 2), l], la_s.at[1], la_r.at[1], (1 - s, to, c)).start()
        return carry

    lax.fori_loop(1, n, send_lat, 0)

    for f in range(2):
        for r in range(2):
            par[0] = rew_in[f, r].astype(F32)
            for p in range(2):
                gb[1 + r, c, 2 * s + f, p] = par[0, pl.ds(p, n, stride=2), :].astype(BF)
    peers = [(1 - s, c), (s, 1 - c), (1 - s, 1 - c)]
    x_copies = []
    for k, (ps, pc) in enumerate(peers):
        mine = gb.at[pl.ds(1, 2), c, pl.ds(2 * s, 2)]
        x_copies.append(remote(mine, mine, xs_s.at[k], xs_r.at[k], (ps, l, pc)))
        x_copies[-1].start()

    w1[...] = jnp.zeros_like(w1)
    wz[...] = jnp.zeros_like(wz)
    xc[...] = jnp.zeros_like(xc)
    lx[...] = jnp.zeros_like(lx)
    h2[...] = jnp.zeros_like(h2)
    sc[...] = jnp.zeros_like(sc)
    copies[0].wait()
    for a in range(3):
        for b in range(3):
            for e in range(3):
                piece = win[a, b, e]
                for rr in range(3):
                    w1[pl.ds((a * 3 + e) * 128 + 16 * (rr + b), 16), pl.ds(rr * c1, c1)] = piece
                for t in range(2):
                    j = t + 2 - a
                    wz[j, e, pl.ds(b * 32 + t * 16, 16), :] = piece

    for copy in x_copies:
        copy.wait_recv()
    r_copies = [
        remote(gb.at[2], gb.at[0], rs_s.at[0], rs_r.at[0], (s, nxt, c)),
        remote(gb.at[1], gb.at[3], rs_s.at[1], rs_r.at[1], (s, prv, c)),
    ]
    for copy in r_copies:
        copy.start()

    def wait_bytes(ref, sem):
        pltpu.make_async_copy(ref, ref, sem).wait()

    wait_bytes(lat.at[pl.ds(0, 2), pl.ds(0, n - 1)], la_r.at[0])
    wait_bytes(lat.at[pl.ds(0, 2)], la_r.at[1])

    for f in range(4):
        x = lat[f].reshape(n, 128)
        for e in range(3):
            moved = (shift_rows(x, 1 - e, row, n) if e != 1 else x).astype(BF)
            for a in range(3):
                t = f + 2 - a
                if t < 4:
                    lx[t, :, pl.ds((a * 3 + e) * 128, 128)] = moved
    big_col = lax.rem(lax.broadcasted_iota(jnp.int32, (rows, c1), 0), n)

    def spread(value, target, r, first, flip):
        for e in range(3):
            step = (e - 1) if flip else (1 - e)
            moved = shift_rows(value, step, big_col, n) if e != 1 else value
            target[r, pl.ds(first, 4), :, pl.ds(e * c1, c1)] = moved.astype(BF).reshape(4, n, c1)

    def norm(v):
        inv = lax.rsqrt(jnp.sum(v * v, axis=1, keepdims=True) / c1 + EPSILON)
        normed = v * inv
        return normed, inv, normed * jax.nn.sigmoid(normed)

    def norm_back(dh, normed, inv):
        sig = jax.nn.sigmoid(normed)
        dn = dh * sig * (1.0 + normed * (1.0 - sig))
        mean = jnp.sum(dn * normed, axis=1, keepdims=True) / c1
        return inv * (dn - normed * mean)

    low_ok = l > 0
    high_ok = l < n - 1
    for rr in range(3):
        seg[...] = jnp.dot(lx[...].reshape(rows, 1152), w1[:, rr * c1:(rr + 1) * c1], preferred_element_type=F32)
        normed, inv, hidden = norm(seg[...])
        if rr == 0:
            hidden = jnp.where(low_ok, hidden, 0.0)
        if rr == 2:
            hidden = jnp.where(high_ok, hidden, 0.0)
        spread(hidden, xc, rr, 2, False)
        if rr == 1:
            n1[...] = normed
            s1[...] = inv
            acc[...] = seg[...]

    copies[1].wait()

    def mid_tap(i, carry):
        a = i // 3
        b = i % 3
        left = xc[b, pl.ds(a, 4)].reshape(rows, 3 * c1)
        acc[...] += jnp.dot(left, wm[a, b].reshape(3 * c1, c1), preferred_element_type=F32)
        return carry

    lax.fori_loop(0, 9, mid_tap, 0)
    normed, inv, hidden = norm(acc[...])
    n2[...] = normed
    s2[...] = inv
    h2[1, pl.ds(2, 4)] = hidden.astype(BF).reshape(4, n, c1)
    mine = h2.at[1, pl.ds(2, 4)]
    h_copies = [
        remote(mine, h2.at[0, pl.ds(2, 4)], hs_s.at[0], hs_r.at[0], (s, nxt, c)),
        remote(mine, h2.at[2, pl.ds(2, 4)], hs_s.at[1], hs_r.at[1], (s, prv, c)),
    ]

    copies[2].wait()
    for copy in r_copies:
        copy.wait_recv()
    col64 = lax.broadcasted_iota(jnp.int32, (n, 96), 0)
    for f in range(4):
        for b in range(3):
            for half in range(2):
                first = gb[2 - b, half, f].astype(F32)
                second = gb[3 - b, half, f].astype(F32)
                if b == 2:
                    first = jnp.where(low_ok, first, 0.0)
                if b == 0:
                    second = jnp.where(high_ok, second, 0.0)
                both = first + second
                even, odd = both[0], both[1]
                whole = even + odd
                cross = odd + shift_rows(even, -1, col64, n)
                back = shift_rows(odd, 1, col64, n) + even
                for e, value in ((0, cross), (1, whole), (2, back)):
                    sc[b, e, f, :, pl.ds(half * 96, 96)] = value.astype(BF)
    up[...] = jnp.zeros_like(up)

    def up_tap(i, carry):
        a = i // 3
        b = i % 3
        for e in range(3):
            left = sc[b, e, pl.ds(2 - a, 4)].reshape(rows, 192)
            up[...] += lax.dot_general(left, wu[a, b, e], NT, preferred_element_type=F32)
        return carry

    lax.fori_loop(0, 9, up_tap, 0)
    grad_two = norm_back(up[...], n2[...], s2[...])
    up[...] = grad_two
    g2[1] = grad_two.astype(BF).reshape(4, n, c1)
    g_copies = [
        remote(g2.at[1], g2.at[0], gs_s.at[0], gs_r.at[0], (s, nxt, c)),
        remote(g2.at[1], g2.at[2], gs_s.at[1], gs_r.at[1], (s, prv, c)),
    ]
    for copy in g_copies:
        copy.start()
    for copy in h_copies:
        copy.start()

    zero_pad = jnp.zeros((2, n, 3 * c1), BF)
    for rr in range(3):
        xc[rr, pl.ds(4, 2)] = zero_pad
    spread(grad_two.astype(BF).astype(F32), xc, 1, 0, True)
    acc[...] = jnp.zeros_like(acc)

    def back_tap(a, b):
        for e in range(3):
            left = xc[2 - b, pl.ds(2 - a, 4), :, pl.ds(e * c1, c1)].reshape(rows, c1)
            acc[...] += lax.dot_general(left, wm[a, b, e], NT, preferred_element_type=F32)

    def own_tap(a, carry):
        back_tap(a, 1)
        return carry

    lax.fori_loop(0, 3, own_tap, 0)
    for copy in g_copies:
        copy.wait_recv()
    for rr, ok in ((0, low_ok), (2, high_ok)):
        halo = g2[rr].reshape(rows, c1).astype(F32)
        spread(jnp.where(ok, halo, 0.0), xc, rr, 0, True)

    def halo_tap(i, carry):
        back_tap(i // 2, (i % 2) * 2)
        return carry

    lax.fori_loop(0, 6, halo_tap, 0)
    grad_one = up[...] + norm_back(acc[...], n1[...], s1[...])
    spread(grad_one.astype(BF).astype(F32), xc, 1, 0, True)
    total = jnp.zeros((n, 128), F32)
    for j in range(4):
        for e in range(3):
            left = xc[1, 2 * s + j, :, pl.ds(e * c1, c1)]
            total = total + lax.dot_general(left, wz[j, e], NT, preferred_element_type=F32)
    zs[...] = total.reshape(n, 1, 128)
    zr[l] = zs[l]

    def send_z(i, carry):
        to = lax.rem(l + i, n)
        remote(zs.at[to], zr.at[l], zsem.at[0], zsem.at[1], (s, to, c)).start()
        return carry

    lax.fori_loop(1, n, send_z, 0)

    for copy in h_copies:
        copy.wait_recv()
    for rr, edge in ((0, l == 0), (2, l == n - 1)):

        @pl.when(edge)
        def _():
            h2[rr] = jnp.zeros_like(h2[rr])

    inter[...] = jnp.zeros_like(inter)
    col128 = lax.rem(lax.broadcasted_iota(jnp.int32, (2 * n, 192), 0), n)

    def dec_tap(a, carry):
        two = pl.ds(2 * s + a, 2)
        for e in range(3):
            inter[e, pl.ds(0, rows)] += jnp.dot(h2[0:2, two].reshape(rows, c1), wu[a, 0, e], preferred_element_type=F32)
            inter[e, pl.ds(0, rows)] += jnp.dot(h2[1:3, two].reshape(rows, c1), wu[a, 2, e], preferred_element_type=F32)
            inter[e, pl.ds(rows, 2 * n)] += jnp.dot(h2[1, two].reshape(2 * n, c1), wu[a, 1, e], preferred_element_type=F32)
        return carry

    lax.fori_loop(0, 3, dec_tap, 0)
    for dy in range(2):
        by_tap = [inter[e, pl.ds(dy * 2 * n, 2 * n)] + inter[e, pl.ds(rows, 2 * n)] for e in range(3)]
        for dx in range(2):
            if dx == 0:
                full = shift_rows(by_tap[0], 1, col128, n) + by_tap[1] + by_tap[2]
            else:
                full = by_tap[0] + by_tap[1] + shift_rows(by_tap[2], -1, col128, n)
            half = jnp.where(c == 0, full[:, :96], full[:, 96:])
            for f in range(2):
                par[f, pl.ds(dx, n, stride=2), :] = half[f * n:(f + 1) * n]
        for f in range(2):
            dec_out[f, dy] = par[f].astype(BF)

    wait_bytes(zr.at[pl.ds(0, n - 1)], zsem.at[1])
    z = zr[...].reshape(n, 128)
    result = shift_rows(z, -1, row, n) + pltpu.roll(z, 128 - 32, axis=1) + pltpu.roll(shift_rows(z, 1, row, n), 128 - 64, axis=1)
    lg_out[...] = result

    wait_bytes(view.at[:, pl.ds(0, n - 1)], la_s.at[0])
    wait_bytes(view, la_s.at[1])
    wait_bytes(zs.at[pl.ds(0, n - 1)], zsem.at[0])
    for copy in x_copies + r_copies + h_copies + g_copies:
        copy.wait_send()


def shards(n, latents, weight_in, weight_mid, weight_up, reward_grad):
    c1 = weight_mid.shape[4]
    c2 = weight_up.shape[4]
    rows = 4 * n
    lat16 = jnp.pad(latents.reshape(2, n, 16), ((0, 0), (0, 0), (0, 112)))
    vm = pltpu.VMEM
    dma = pltpu.SemaphoreType.DMA
    any_spec = pl.BlockSpec(memory_space=pl.ANY)
    vm_spec = pl.BlockSpec(memory_space=vm)
    decoded, grad = pl.pallas_call(
        functools.partial(kernel, n),
        out_shape=(
            jax.ShapeDtypeStruct((2, 2, 2 * n, c2 // 2), BF),
            jax.ShapeDtypeStruct((n, 128), F32),
        ),
        in_specs=[vm_spec, vm_spec, any_spec, any_spec, any_spec],
        out_specs=(vm_spec, vm_spec),
        scratch_shapes=[
            vm((3, 3, 3, c1, c1), BF),
            vm((3, 3, 3, c1, c2), BF),
            vm((3, 3, 3, 16, c1), BF),
            vm((1152, 3 * c1), BF),
            vm((4, 3, 128, c1), BF),
            vm((2, 2 * n, c2 // 2), F32),
            vm((4, 2, 4, 2, n, c2 // 2), BF),
            vm((2, n, 1, 128), F32),
            vm((4, n, 1, 128), F32),
            vm((4, n, 1152), BF),
            vm((3, 6, n, 3 * c1), BF),
            vm((3, 6, n, c1), BF),
            vm((3, 4, n, c1), BF),
            vm((3, 3, 6, n, c2), BF),
            vm((rows, c1), F32),
            vm((rows, c1), F32),
            vm((rows, 1), F32),
            vm((rows, c1), F32),
            vm((rows, 1), F32),
            vm((rows, c1), F32),
            vm((n, 1, 128), F32),
            vm((n, 1, 128), F32),
            vm((rows, c1), F32),
            vm((3, 6 * n, c2), F32),
            dma((3,)), dma((3,)), dma((3,)), dma((2,)), dma((2,)), dma((2,)), dma((2,)),
            dma((2,)), dma((2,)), dma((2,)), dma((2,)), dma((2,)),
        ],
        compiler_params=pltpu.CompilerParams(has_side_effects=True, vmem_limit_bytes=60 * 1024 * 1024),
    )(lat16, reward_grad, weight_in, weight_mid, weight_up)
    latent_grad = grad[:, :32].reshape(n, 2, 16).transpose(1, 0, 2).reshape(2, n, 1, 16)
    return decoded, latent_grad


def solution(mesh):
    return jax.shard_map(
        functools.partial(shards, mesh.shape["slab"]),
        mesh=mesh,
        in_specs=(P("sec", None, "slab", None), P(), P(), P(), P("sec", "slab", None, "ch")),
        out_specs=(P("sec", "slab", None, "ch"), P("sec", None, "slab", None)),
        check_vma=False,
    )
```

profile of v0, /device:TPU:1, one launch (start us, length us, event | category | flops | bytes accessed | tf_op | source)
XLA Modules:
  0.0 72.3 jit_solution(933065300355333725)
XLA Ops:
  0.6 0.8 %copy.12 = bf16[2,64,1,16]{3,1,0,2:T(8,128)(2,1)S(1)} copy(bf16[2,64,1,16]{1,3,2,0:T(8,128)(2,1)} %param.5) | data formatting | bytes 8192 | tf_op args[0]
  1.4 0.6 pad.4.lat_in
  2.0 1.6 %copy.13.rew_in = bf16[2,2,128,96]{3,2,1,0:T(8,128)(2,1)} copy(bf16[2,2,128,96]{2,3,1,0:T(8,128)(2,1)} %param.9) | data formatting | bytes 196608 | tf_op args[4]
  3.7 8.2 %copy.14.wu_hbm = bf16[3,3,3,384,192]{4,3,2,1,0:T(8,128)(2,1)} copy(bf16[3,3,3,384,192]{3,4,2,1,0:T(8,128)(2,1)} %param.8) | data formatting | bytes 7962624 | tf_op args[3]
  11.9 57.3 %shard_map.68 = (bf16[2,2,128,96]{3,2,1,0:T(8,128)(2,1)}, f32[64,128]{1,0:T(8,128)}) custom-call(bf16[2,64,128]{2,1,0:T(8,128)(2,1)} %pad.4.lat_in, bf16[2,2,128,96]{3,2,1,0:T(8,128)(2,1)} %copy.13.rew_in, bf16[3,3,3,16,384]{4,3,2,1,0:T(8,128)(2,1)} %win_hbm.1, bf16[3,3,3,384,384]{4,3,2,1,0:T(8,128)(2,1)} %wm_hbm.1, bf16[3,3,3,384,192]{4,3,2,1,0:T(8,128)(2,1)} %copy.14.wu_hbm), custom_call_target="tpu_custom_call" | custom-call | tf_op jit(solution)/shard_map/pallas_call | solution.py:318
  69.2 1.6 %copy.16 = bf16[2,2,128,96]{2,3,1,0:T(8,128)(2,1)} copy(bf16[2,2,128,96]{3,2,1,0:T(8,128)(2,1)} %get-tuple-element.8) | data formatting | bytes 196608
  70.8 1.4 %copy.15 = f32[64,32]{0,1:T(8,128)} copy(f32[64,32]{1,0:T(8,128)} %bitcast.10) | data formatting | bytes 16384 | tf_op jit(solution)/shard_map/slice | solution.py:356
where the time goes:
time: 72.7 us; the launch traced here: 72.3 us
  Pallas kernels  57.3 us (79%)
  local copies, waits for them, and re-layouts  14.3 us (20%)
    pallas_call x1, Pallas kernels, shards(): pl.pallas_call(functools.partial(kernel, n), out_shape=(jax.ShapeDtypeStr...  57.3 us
    unnamed x4, local copies, waits for them, and re-layouts  12.2 us

commit v1 on v0

--- a/solution.py
+++ b/solution.py
@@ -21,9 +21,9 @@
     return jnp.where(col >= width + step, 0.0, rolled)
 
 
-def kernel(n, lat_in, rew_in, win_hbm, wm_hbm, wu_hbm, dec_out, lg_out,
-           wm, wu, win, w1, wz, par, gb, view, lat, lx, xc, h2, g2, sc, seg, n1, s1, n2, s2, acc, zs, zr, up, inter,
-           wsem, xs_s, xs_r, rs_s, rs_r, la_s, la_r, hs_s, hs_r, gs_s, gs_r, zsem):
+def kernel(n, lat_in, rew_hbm, win_hbm, wm_hbm, wu_hbm, dec_out, lg_out,
+           wm, wu, win, w1, wz, bsel, par, gb, view, lat, lx, xc, h2, g2, sc, seg, n1, s1, n2, s2, acc, zs, zr, up, inter,
+           wsem, own_sem, xs_s, xs_r, rs_s, rs_r, la_s, la_r, hs_s, hs_r, gs_s, gs_r, zsem):
     s = lax.axis_index("sec")
     l = lax.axis_index("slab")
     c = lax.axis_index("ch")
@@ -31,61 +31,54 @@
     prv = lax.rem(l + n - 1, n)
     rows = 4 * n
     c1 = wm.shape[3]
+    c2 = wu.shape[3]
 
     copies = [
         pltpu.make_async_copy(win_hbm, win, wsem.at[0]),
         pltpu.make_async_copy(wm_hbm, wm, wsem.at[1]),
         pltpu.make_async_copy(wu_hbm, wu, wsem.at[2]),
     ]
-    for copy in copies:
+    own = pltpu.make_async_copy(rew_hbm, gb.at[pl.ds(2 * s, 2), pl.ds(1, 2), c], own_sem)
+    for copy in copies[:1] + [own] + copies[1:]:
         copy.start()
+
+    barrier = pltpu.get_barrier_semaphore()
+
+    def greet(ps, to, pc):
+        pl.semaphore_signal(barrier, inc=1, device_id=(ps, to, pc), device_id_type=MESH)
+
+    def greet_all(i, carry):
+        to = lax.rem(l + i, n)
+        greet(s, to, c)
+        greet(1 - s, to, c)
+        return carry
+
+    peers = [(1 - s, c), (s, 1 - c), (1 - s, 1 - c)]
+    for ps, pc in peers:
+        greet(ps, l, pc)
+    lax.fori_loop(1, n, greet_all, 0)
 
     def remote(src, dst, ss, rs, dev):
         return pltpu.make_async_remote_copy(src_ref=src, dst_ref=dst, send_sem=ss, recv_sem=rs, device_id=dev, device_id_type=MESH)
 
-    lane = lax.broadcasted_iota(jnp.int32, (n, 128), 1)
     row = lax.broadcasted_iota(jnp.int32, (n, 128), 0)
     for f in range(2):
-        x = lat_in[f].astype(F32)
-        total = jnp.zeros((n, 128), F32)
-        for r in range(5):
-            moved = shift_rows(x, 2 - r, row, n) if r != 2 else x
-            if r:
-                moved = pltpu.roll(moved, 16 * r, axis=1)
-            total = total + moved
-        view[f] = total.reshape(n, 1, 128)
-
-    for i in range(2):
-        lat[2 * s + i, l] = view[i, l]
-    other = remote(view.at[:, l], lat.at[pl.ds(2 * s, 2), l], la_s.at[1], la_r.at[1], (1 - s, l, c))
-    other.start()
-
-    def send_lat(i, carry):
-        to = lax.rem(l + i, n)
-        remote(view.at[:, to], lat.at[pl.ds(2 * s, 2), l], la_s.at[0], la_r.at[0], (s, to, c)).start()
-        remote(view.at[:, to], lat.at[pl.ds(2 * s, 2), l], la_s.at[1], la_r.at[1], (1 - s, to, c)).start()
-        return carry
-
-    lax.fori_loop(1, n, send_lat, 0)
-
-    for f in range(2):
-        for r in range(2):
-            par[0] = rew_in[f, r].astype(F32)
-            for p in range(2):
-                gb[1 + r, c, 2 * s + f, p] = par[0, pl.ds(p, n, stride=2), :].astype(BF)
-    peers = [(1 - s, c), (s, 1 - c), (1 - s, 1 - c)]
-    x_copies = []
-    for k, (ps, pc) in enumerate(peers):
-        mine = gb.at[pl.ds(1, 2), c, pl.ds(2 * s, 2)]
-        x_copies.append(remote(mine, mine, xs_s.at[k], xs_r.at[k], (ps, l, pc)))
-        x_copies[-1].start()
-
+        x = jnp.concatenate([lat_in[f].astype(F32), jnp.zeros((16, 128 - n), F32)], axis=1)
+        stack = [pltpu.roll(x, (2 - r) % 128, axis=1) if r != 2 else x for r in range(5)]
+        both = jnp.concatenate(stack + [jnp.zeros((48, 128), F32)], axis=0)
+        view[f] = both.T[:n].reshape(n, 1, 128)
+
+    pick_row = lax.broadcasted_iota(jnp.int32, (n, 2 * n), 0)
+    pick_col = lax.broadcasted_iota(jnp.int32, (n, 2 * n), 1)
+    for e in range(3):
+        delta = pick_col - 2 * pick_row - (1 - e)
+        bsel[pl.ds(e * n, n)] = jnp.where((delta == 0) | (delta == 1), 1.0, 0.0).astype(BF)
     w1[...] = jnp.zeros_like(w1)
     wz[...] = jnp.zeros_like(wz)
-    xc[...] = jnp.zeros_like(xc)
+    xc[:, pl.ds(0, 2)] = jnp.zeros((3, 2, n, 3 * c1), BF)
     lx[...] = jnp.zeros_like(lx)
-    h2[...] = jnp.zeros_like(h2)
-    sc[...] = jnp.zeros_like(sc)
+    h2[:, pl.ds(0, 2)] = jnp.zeros((3, 2, n, c1), BF)
+    sc[:, :, pl.ds(4, 2)] = jnp.zeros((3, 3, 2, n, c2), BF)
     copies[0].wait()
     for a in range(3):
         for b in range(3):
@@ -96,18 +89,28 @@
                 for t in range(2):
                     j = t + 2 - a
                     wz[j, e, pl.ds(b * 32 + t * 16, 16), :] = piece
-
-    for copy in x_copies:
-        copy.wait_recv()
-    r_copies = [
-        remote(gb.at[2], gb.at[0], rs_s.at[0], rs_r.at[0], (s, nxt, c)),
-        remote(gb.at[1], gb.at[3], rs_s.at[1], rs_r.at[1], (s, prv, c)),
-    ]
-    for copy in r_copies:
-        copy.start()
+    for i in range(2):
+        lat[2 * s + i, l] = view[i, l]
+
+    pl.semaphore_wait(barrier, 2 * n + 1)
 
     def wait_bytes(ref, sem):
         pltpu.make_async_copy(ref, ref, sem).wait()
+
+    other = remote(view.at[:, l], lat.at[pl.ds(2 * s, 2), l], la_s.at[1], la_r.at[1], (1 - s, l, c))
+    other.start()
+
+    def send_lat(i, carry):
+        to = lax.rem(l + i, n)
+        remote(view.at[:, to], lat.at[pl.ds(2 * s, 2), l], la_s.at[0], la_r.at[0], (s, to, c)).start()
+        remote(view.at[:, to], lat.at[pl.ds(2 * s, 2), l], la_s.at[1], la_r.at[1], (1 - s, to, c)).start()
+        return carry
+
+    lax.fori_loop(1, n, send_lat, 0)
+    x_copies = []
+    for k, (ps, pc) in enumerate(peers):
+        x_copies.append(remote(rew_hbm, gb.at[pl.ds(2 * s, 2), pl.ds(1, 2), c], xs_s.at[k], xs_r.at[k], (ps, l, pc)))
+        x_copies[-1].start()
 
     wait_bytes(lat.at[pl.ds(0, 2), pl.ds(0, n - 1)], la_r.at[0])
     wait_bytes(lat.at[pl.ds(0, 2)], la_r.at[1])
@@ -154,6 +157,16 @@
             s1[...] = inv
             acc[...] = seg[...]
 
+    own.wait()
+    for copy in x_copies:
+        copy.wait_recv()
+    r_copies = [
+        remote(gb.at[:, 2], gb.at[:, 0], rs_s.at[0], rs_r.at[0], (s, nxt, c)),
+        remote(gb.at[:, 1], gb.at[:, 3], rs_s.at[1], rs_r.at[1], (s, prv, c)),
+    ]
+    for copy in r_copies:
+        copy.start()
+
     copies[1].wait()
 
     def mid_tap(i, carry):
@@ -173,35 +186,33 @@
         remote(mine, h2.at[0, pl.ds(2, 4)], hs_s.at[0], hs_r.at[0], (s, nxt, c)),
         remote(mine, h2.at[2, pl.ds(2, 4)], hs_s.at[1], hs_r.at[1], (s, prv, c)),
     ]
+    for copy in h_copies:
+        copy.start()
 
     copies[2].wait()
     for copy in r_copies:
         copy.wait_recv()
-    col64 = lax.broadcasted_iota(jnp.int32, (n, 96), 0)
+    for i, edge in ((0, l == 0), (3, l == n - 1)):
+
+        @pl.when(edge)
+        def _():
+            gb[:, i] = jnp.zeros_like(gb[:, i])
+
     for f in range(4):
         for b in range(3):
-            for half in range(2):
-                first = gb[2 - b, half, f].astype(F32)
-                second = gb[3 - b, half, f].astype(F32)
-                if b == 2:
-                    first = jnp.where(low_ok, first, 0.0)
-                if b == 0:
-                    second = jnp.where(high_ok, second, 0.0)
-                both = first + second
-                even, odd = both[0], both[1]
-                whole = even + odd
-                cross = odd + shift_rows(even, -1, col64, n)
-                back = shift_rows(odd, 1, col64, n) + even
-                for e, value in ((0, cross), (1, whole), (2, back)):
-                    sc[b, e, f, :, pl.ds(half * 96, 96)] = value.astype(BF)
+            first = lax.dot_general(bsel[...], gb[f, 2 - b].reshape(c2, 2 * n), NT, preferred_element_type=F32)
+            second = lax.dot_general(bsel[...], gb[f, 3 - b].reshape(c2, 2 * n), NT, preferred_element_type=F32)
+            pooled = (first + second).astype(BF)
+            for e in range(3):
+                sc[b, e, f] = pooled[e * n:(e + 1) * n]
     up[...] = jnp.zeros_like(up)
 
     def up_tap(i, carry):
         a = i // 3
         b = i % 3
         for e in range(3):
-            left = sc[b, e, pl.ds(2 - a, 4)].reshape(rows, 192)
-            up[...] += lax.dot_general(left, wu[a, b, e], NT, preferred_element_type=F32)
+            left = sc[b, e, pl.ds(2 - a, 4)].reshape(rows, c2)
+            up[...] += jnp.dot(left, wu[a, b, e], preferred_element_type=F32)
         return carry
 
     lax.fori_loop(0, 9, up_tap, 0)
@@ -214,8 +225,6 @@
     ]
     for copy in g_copies:
         copy.start()
-    for copy in h_copies:
-        copy.start()
 
     zero_pad = jnp.zeros((2, n, 3 * c1), BF)
     for rr in range(3):
@@ -270,14 +279,15 @@
             h2[rr] = jnp.zeros_like(h2[rr])
 
     inter[...] = jnp.zeros_like(inter)
-    col128 = lax.rem(lax.broadcasted_iota(jnp.int32, (2 * n, 192), 0), n)
+    col128 = lax.rem(lax.broadcasted_iota(jnp.int32, (2 * n, c2 // 2), 0), n)
 
     def dec_tap(a, carry):
         two = pl.ds(2 * s + a, 2)
-        for e in range(3):
-            inter[e, pl.ds(0, rows)] += jnp.dot(h2[0:2, two].reshape(rows, c1), wu[a, 0, e], preferred_element_type=F32)
-            inter[e, pl.ds(0, rows)] += jnp.dot(h2[1:3, two].reshape(rows, c1), wu[a, 2, e], preferred_element_type=F32)
-            inter[e, pl.ds(rows, 2 * n)] += jnp.dot(h2[1, two].reshape(2 * n, c1), wu[a, 1, e], preferred_element_type=F32)
+        half = pl.ds(c * (c2 // 2), c2 // 2)
+        for e in range(3):
+            inter[e, pl.ds(0, rows)] += lax.dot_general(h2[0:2, two].reshape(rows, c1), wu[a, 0, e, half], NT, preferred_element_type=F32)
+            inter[e, pl.ds(0, rows)] += lax.dot_general(h2[1:3, two].reshape(rows, c1), wu[a, 2, e, half], NT, preferred_element_type=F32)
+            inter[e, pl.ds(rows, 2 * n)] += lax.dot_general(h2[1, two].reshape(2 * n, c1), wu[a, 1, e, half], NT, preferred_element_type=F32)
         return carry
 
     lax.fori_loop(0, 3, dec_tap, 0)
@@ -288,16 +298,15 @@
                 full = shift_rows(by_tap[0], 1, col128, n) + by_tap[1] + by_tap[2]
             else:
                 full = by_tap[0] + by_tap[1] + shift_rows(by_tap[2], -1, col128, n)
-            half = jnp.where(c == 0, full[:, :96], full[:, 96:])
             for f in range(2):
-                par[f, pl.ds(dx, n, stride=2), :] = half[f * n:(f + 1) * n]
+                par[f, pl.ds(dx, n, stride=2), :] = full[f * n:(f + 1) * n]
         for f in range(2):
-            dec_out[f, dy] = par[f].astype(BF)
+            dec_out[f, dy] = par[f].T.astype(BF)
 
     wait_bytes(zr.at[pl.ds(0, n - 1)], zsem.at[1])
     z = zr[...].reshape(n, 128)
     result = shift_rows(z, -1, row, n) + pltpu.roll(z, 128 - 32, axis=1) + pltpu.roll(shift_rows(z, 1, row, n), 128 - 64, axis=1)
-    lg_out[...] = result
+    lg_out[...] = result.T[:32].reshape(2, 16, n)
 
     wait_bytes(view.at[:, pl.ds(0, n - 1)], la_s.at[0])
     wait_bytes(view, la_s.at[1])
@@ -310,7 +319,6 @@
     c1 = weight_mid.shape[4]
     c2 = weight_up.shape[4]
     rows = 4 * n
-    lat16 = jnp.pad(latents.reshape(2, n, 16), ((0, 0), (0, 0), (0, 112)))
     vm = pltpu.VMEM
     dma = pltpu.SemaphoreType.DMA
     any_spec = pl.BlockSpec(memory_space=pl.ANY)
@@ -318,19 +326,20 @@
     decoded, grad = pl.pallas_call(
         functools.partial(kernel, n),
         out_shape=(
-            jax.ShapeDtypeStruct((2, 2, 2 * n, c2 // 2), BF),
-            jax.ShapeDtypeStruct((n, 128), F32),
+            jax.ShapeDtypeStruct((2, 2, c2 // 2, 2 * n), BF),
+            jax.ShapeDtypeStruct((2, 16, n), F32),
         ),
-        in_specs=[vm_spec, vm_spec, any_spec, any_spec, any_spec],
+        in_specs=[vm_spec, any_spec, any_spec, any_spec, any_spec],
         out_specs=(vm_spec, vm_spec),
         scratch_shapes=[
             vm((3, 3, 3, c1, c1), BF),
-            vm((3, 3, 3, c1, c2), BF),
+            vm((3, 3, 3, c2, c1), BF),
             vm((3, 3, 3, 16, c1), BF),
             vm((1152, 3 * c1), BF),
             vm((4, 3, 128, c1), BF),
+            vm((3 * n, 2 * n), BF),
             vm((2, 2 * n, c2 // 2), F32),
-            vm((4, 2, 4, 2, n, c2 // 2), BF),
+            vm((4, 4, 2, c2 // 2, 2 * n), BF),
             vm((2, n, 1, 128), F32),
             vm((4, n, 1, 128), F32),
             vm((4, n, 1152), BF),
@@ -347,14 +356,13 @@
             vm((n, 1, 128), F32),
             vm((n, 1, 128), F32),
             vm((rows, c1), F32),
-            vm((3, 6 * n, c2), F32),
-            dma((3,)), dma((3,)), dma((3,)), dma((2,)), dma((2,)), dma((2,)), dma((2,)),
+            vm((3, 6 * n, c2 // 2), F32),
+            dma((3,)), dma, dma((3,)), dma((3,)), dma((2,)), dma((2,)), dma((2,)), dma((2,)),
             dma((2,)), dma((2,)), dma((2,)), dma((2,)), dma((2,)),
         ],
-        compiler_params=pltpu.CompilerParams(has_side_effects=True, vmem_limit_bytes=60 * 1024 * 1024),
-    )(lat16, reward_grad, weight_in, weight_mid, weight_up)
-    latent_grad = grad[:, :32].reshape(n, 2, 16).transpose(1, 0, 2).reshape(2, n, 1, 16)
-    return decoded, latent_grad
+        compiler_params=pltpu.CompilerParams(has_side_effects=True, collective_id=0, vmem_limit_bytes=60 * 1024 * 1024),
+    )(latents.reshape(2, n, 16).transpose(0, 2, 1), reward_grad.transpose(0, 1, 3, 2), weight_in, weight_mid, weight_up.transpose(0, 1, 2, 4, 3))
+    return decoded.transpose(0, 1, 3, 2), grad.transpose(0, 2, 1).reshape(2, n, 1, 16)
 
 
 def solution(mesh):

time: 72.7 us -> 52.9 us (0.73)
  local copies, waits for them, and re-layouts: 14.3 us -> 2.86 us
  Pallas kernels: 57.3 us -> 49.1 us
    unnamed x4 -> x2, local copies, waits for them, and re-layouts: 12.2 us -> 2.86 us
    pallas_call x1, Pallas kernels: 57.3 us -> 49.1 us  [shards(): pl.pallas_call(functools.partial(kernel, n), out_shape=(jax.ShapeDtypeStr...]
    slice x1 -> x0, local copies, waits for them, and re-layouts: 1.44 us -> none  [shards(): grad[:, :32].reshape(n, 2, 16).transpose(1, 0, 2).reshape(2, n, 1, 16)]
where the time goes in v1:
time: 52.9 us; the launch traced here: 52.6 us
  Pallas kernels  49.1 us (93%)
  local copies, waits for them, and re-layouts  2.86 us (5%)
  between operations  0.64 us (1%)
    pallas_call x1, Pallas kernels, shards(): pl.pallas_call(functools.partial(kernel, n), out_shape=(jax.ShapeDtypeStr...  49.1 us
    unnamed x2, local copies, waits for them, and re-layouts  2.86 us

profile of v1, /device:TPU:1, one launch (start us, length us, event | category | flops | bytes accessed | tf_op | source)
XLA Modules:
  0.0 52.6 jit_solution(17278339431808261789)
XLA Ops:
  0.6 49.1 %shard_map.68 = (bf16[2,2,96,128]{3,2,1,0:T(8,128)(2,1)}, f32[2,16,64]{2,1,0:T(8,128)}) custom-call(bf16[2,16,64]{2,1,0:T(8,128)(2,1)} %bitcast.15, bf16[2,2,96,128]{3,2,1,0:T(8,128)(2,1)} %bitcast.12, bf16[3,3,3,16,384]{4,3,2,1,0:T(8,128)(2,1)} %win_hbm.1, bf16[3,3,3,384,384]{4,3,2,1,0:T(8,128)(2,1)} %wm_hbm.1, bf16[3,3,3,192,384]{4,3,2,1,0:T(8,128)(2,1)} %bitcast.11), custom_call_target="tpu_custom_call" | custom-call | tf_op jit(solution)/shard_map/pallas_call | solution.py:326
  49.7 1.5 %copy.10 = bf16[2,2,128,96]{2,3,1,0:T(8,128)(2,1)} copy(bf16[2,2,128,96]{2,3,1,0:T(8,128)(2,1)} %bitcast.13) | data formatting | bytes 196608
  51.3 1.3 %copy.11 = f32[2,64,1,16]{1,3,2,0:T(8,128)} copy(f32[2,64,1,16]{1,3,2,0:T(8,128)} %bitcast.14) | data formatting | bytes 16384

commit v2 on v1

--- a/solution.py
+++ b/solution.py
@@ -47,16 +47,24 @@
     def greet(ps, to, pc):
         pl.semaphore_signal(barrier, inc=1, device_id=(ps, to, pc), device_id_type=MESH)
 
-    def greet_all(i, carry):
-        to = lax.rem(l + i, n)
+    chunk = 9 if (n - 1) % 9 == 0 else n - 1
+
+    def each_partner(act):
+        def step(k, carry):
+            for i in range(chunk):
+                act(lax.rem(l + k * chunk + (1 + i), n))
+            return carry
+
+        lax.fori_loop(0, (n - 1) // chunk, step, 0)
+
+    def greet_all(to):
         greet(s, to, c)
         greet(1 - s, to, c)
-        return carry
 
     peers = [(1 - s, c), (s, 1 - c), (1 - s, 1 - c)]
     for ps, pc in peers:
         greet(ps, l, pc)
-    lax.fori_loop(1, n, greet_all, 0)
+    each_partner(greet_all)
 
     def remote(src, dst, ss, rs, dev):
         return pltpu.make_async_remote_copy(src_ref=src, dst_ref=dst, send_sem=ss, recv_sem=rs, device_id=dev, device_id_type=MESH)
@@ -97,20 +105,28 @@
     def wait_bytes(ref, sem):
         pltpu.make_async_copy(ref, ref, sem).wait()
 
-    other = remote(view.at[:, l], lat.at[pl.ds(2 * s, 2), l], la_s.at[1], la_r.at[1], (1 - s, l, c))
-    other.start()
-
-    def send_lat(i, carry):
-        to = lax.rem(l + i, n)
-        remote(view.at[:, to], lat.at[pl.ds(2 * s, 2), l], la_s.at[0], la_r.at[0], (s, to, c)).start()
-        remote(view.at[:, to], lat.at[pl.ds(2 * s, 2), l], la_s.at[1], la_r.at[1], (1 - s, to, c)).start()
-        return carry
-
-    lax.fori_loop(1, n, send_lat, 0)
     x_copies = []
     for k, (ps, pc) in enumerate(peers):
         x_copies.append(remote(rew_hbm, gb.at[pl.ds(2 * s, 2), pl.ds(1, 2), c], xs_s.at[k], xs_r.at[k], (ps, l, pc)))
         x_copies[-1].start()
+
+    def send_lat(to):
+        remote(view.at[:, to], lat.at[pl.ds(2 * s, 2), l], la_s.at[0], la_r.at[0], (s, to, c)).start()
+        remote(view.at[:, to], lat.at[pl.ds(2 * s, 2), l], la_s.at[1], la_r.at[1], (1 - s, to, c)).start()
+
+    each_partner(send_lat)
+    other = remote(view.at[:, l], lat.at[pl.ds(2 * s, 2), l], la_s.at[1], la_r.at[1], (1 - s, l, c))
+    other.start()
+
+    own.wait()
+    for copy in x_copies:
+        copy.wait_recv()
+    r_copies = [
+        remote(gb.at[:, 2], gb.at[:, 0], rs_s.at[0], rs_r.at[0], (s, nxt, c)),
+        remote(gb.at[:, 1], gb.at[:, 3], rs_s.at[1], rs_r.at[1], (s, prv, c)),
+    ]
+    for copy in r_copies:
+        copy.start()
 
     wait_bytes(lat.at[pl.ds(0, 2), pl.ds(0, n - 1)], la_r.at[0])
     wait_bytes(lat.at[pl.ds(0, 2)], la_r.at[1])
@@ -157,16 +173,6 @@
             s1[...] = inv
             acc[...] = seg[...]
 
-    own.wait()
-    for copy in x_copies:
-        copy.wait_recv()
-    r_copies = [
-        remote(gb.at[:, 2], gb.at[:, 0], rs_s.at[0], rs_r.at[0], (s, nxt, c)),
-        remote(gb.at[:, 1], gb.at[:, 3], rs_s.at[1], rs_r.at[1], (s, prv, c)),
-    ]
-    for copy in r_copies:
-        copy.start()
-
     copies[1].wait()
 
     def mid_tap(i, carry):
@@ -263,12 +269,10 @@
     zs[...] = total.reshape(n, 1, 128)
     zr[l] = zs[l]
 
-    def send_z(i, carry):
-        to = lax.rem(l + i, n)
+    def send_z(to):
         remote(zs.at[to], zr.at[l], zsem.at[0], zsem.at[1], (s, to, c)).start()
-        return carry
-
-    lax.fori_loop(1, n, send_z, 0)
+
+    each_partner(send_z)
 
     for copy in h_copies:
         copy.wait_recv()
@@ -313,6 +317,11 @@
     wait_bytes(zs.at[pl.ds(0, n - 1)], zsem.at[0])
     for copy in x_copies + r_copies + h_copies + g_copies:
         copy.wait_send()
+
+
+def close_kernel(dec_in, lg_in, dec_out, lg_out):
+    dec_out[...] = dec_in[...]
+    lg_out[...] = lg_in[...]
 
 
 def shards(n, latents, weight_in, weight_mid, weight_up, reward_grad):
@@ -362,6 +371,13 @@
         ],
         compiler_params=pltpu.CompilerParams(has_side_effects=True, collective_id=0, vmem_limit_bytes=60 * 1024 * 1024),
     )(latents.reshape(2, n, 16).transpose(0, 2, 1), reward_grad.transpose(0, 1, 3, 2), weight_in, weight_mid, weight_up.transpose(0, 1, 2, 4, 3))
+    decoded, grad = pl.pallas_call(
+        close_kernel,
+        out_shape=(
+            jax.ShapeDtypeStruct(decoded.shape, BF),
+            jax.ShapeDtypeStruct(grad.shape, F32),
+        ),
+    )(decoded, grad)
     return decoded.transpose(0, 1, 3, 2), grad.transpose(0, 2, 1).reshape(2, n, 1, 16)
 
 

time: 52.9 us -> 50.2 us (0.949)
  local copies, waits for them, and re-layouts: 2.86 us -> 0 us
    unnamed x2 -> x0, local copies, waits for them, and re-layouts: 2.86 us -> none
    pallas_call x0 -> x1, Pallas kernels: none -> 1.55 us  [shards(): pl.pallas_call(close_kernel, out_shape=(jax.ShapeDtypeStruct(decoded.shap...]
    pallas_call x1, Pallas kernels: 49.1 us -> 47.9 us  [shards(): pl.pallas_call(functools.partial(kernel, n), out_shape=(jax.ShapeDtypeStr...]
where the time goes in v2:
time: 50.2 us; the launch traced here: 50.1 us
  Pallas kernels  49.4 us (98%)
  between operations  0.64 us (1%)
    pallas_call x1, Pallas kernels, shards(): pl.pallas_call(functools.partial(kernel, n), out_shape=(jax.ShapeDtypeStr...  47.9 us
    pallas_call x1, Pallas kernels, shards(): pl.pallas_call(close_kernel, out_shape=(jax.ShapeDtypeStruct(decoded.shap...  1.55 us

profile of v2, /device:TPU:1, one launch (start us, length us, event | category | flops | bytes accessed | tf_op | source)
XLA Modules:
  0.0 50.1 jit_solution(2564630999161759672)
XLA Ops:
  0.6 47.9 %shard_map.68 = (bf16[2,2,96,128]{3,2,1,0:T(8,128)(2,1)}, f32[2,16,64]{2,1,0:T(8,128)}) custom-call(bf16[2,16,64]{2,1,0:T(8,128)(2,1)} %bitcast.13, bf16[2,2,96,128]{3,2,1,0:T(8,128)(2,1)} %bitcast.12, bf16[3,3,3,16,384]{4,3,2,1,0:T(8,128)(2,1)} %win_hbm.1, bf16[3,3,3,384,384]{4,3,2,1,0:T(8,128)(2,1)} %wm_hbm.1, bf16[3,3,3,192,384]{4,3,2,1,0:T(8,128)(2,1)} %bitcast.11), custom_call_target="tpu_custom_call" | custom-call | tf_op jit(solution)/shard_map/pallas_call | solution.py:335
  48.5 1.5 %shard_map.69 = (bf16[2,2,96,128]{3,2,1,0:T(8,128)(2,1)}, f32[2,16,64]{2,1,0:T(8,128)}) custom-call(bf16[2,2,96,128]{3,2,1,0:T(8,128)(2,1)} %get-tuple-element.6.dec_in, f32[2,16,64]{2,1,0:T(8,128)} %get-tuple-element.7.lg_in), custom_call_target="tpu_custom_call" | custom-call | tf_op jit(solution)/shard_map/pallas_call | solution.py:374

commit v3 on v2

--- a/solution.py
+++ b/solution.py
@@ -83,10 +83,8 @@
         bsel[pl.ds(e * n, n)] = jnp.where((delta == 0) | (delta == 1), 1.0, 0.0).astype(BF)
     w1[...] = jnp.zeros_like(w1)
     wz[...] = jnp.zeros_like(wz)
-    xc[:, pl.ds(0, 2)] = jnp.zeros((3, 2, n, 3 * c1), BF)
     lx[...] = jnp.zeros_like(lx)
     h2[:, pl.ds(0, 2)] = jnp.zeros((3, 2, n, c1), BF)
-    sc[:, :, pl.ds(4, 2)] = jnp.zeros((3, 3, 2, n, c2), BF)
     copies[0].wait()
     for a in range(3):
         for b in range(3):
@@ -175,14 +173,14 @@
 
     copies[1].wait()
 
-    def mid_tap(i, carry):
-        a = i // 3
-        b = i % 3
-        left = xc[b, pl.ds(a, 4)].reshape(rows, 3 * c1)
-        acc[...] += jnp.dot(left, wm[a, b].reshape(3 * c1, c1), preferred_element_type=F32)
+    def mid_taps(b, carry):
+        for a in range(3):
+            left = xc[b, pl.ds(2, 2 + a)].reshape((2 + a) * n, 3 * c1)
+            part = pl.ds((2 - a) * n, (2 + a) * n)
+            acc[part] += jnp.dot(left, wm[a, b].reshape(3 * c1, c1), preferred_element_type=F32)
         return carry
 
-    lax.fori_loop(0, 9, mid_tap, 0)
+    lax.fori_loop(0, 3, mid_taps, 0)
     normed, inv, hidden = norm(acc[...])
     n2[...] = normed
     s2[...] = inv
@@ -196,32 +194,40 @@
         copy.start()
 
     copies[2].wait()
-    for copy in r_copies:
-        copy.wait_recv()
-    for i, edge in ((0, l == 0), (3, l == n - 1)):
-
-        @pl.when(edge)
-        def _():
-            gb[:, i] = jnp.zeros_like(gb[:, i])
-
-    for f in range(4):
-        for b in range(3):
+
+    def pool(b):
+        for f in range(4):
             first = lax.dot_general(bsel[...], gb[f, 2 - b].reshape(c2, 2 * n), NT, preferred_element_type=F32)
             second = lax.dot_general(bsel[...], gb[f, 3 - b].reshape(c2, 2 * n), NT, preferred_element_type=F32)
             pooled = (first + second).astype(BF)
             for e in range(3):
                 sc[b, e, f] = pooled[e * n:(e + 1) * n]
+
+    def up_taps(b):
+        for a in range(3):
+            for e in range(3):
+                left = sc[b, e, pl.ds(2 - a, 2 + a)].reshape((2 + a) * n, c2)
+                up[pl.ds(0, (2 + a) * n)] += jnp.dot(left, wu[a, b, e], preferred_element_type=F32)
+
     up[...] = jnp.zeros_like(up)
-
-    def up_tap(i, carry):
-        a = i // 3
-        b = i % 3
-        for e in range(3):
-            left = sc[b, e, pl.ds(2 - a, 4)].reshape(rows, c2)
-            up[...] += jnp.dot(left, wu[a, b, e], preferred_element_type=F32)
+    pool(1)
+    up_taps(1)
+    for copy in r_copies:
+        copy.wait_recv()
+    for i, edge in ((0, l == 0), (3, l == n - 1)):
+
+        @pl.when(edge)
+        def _():
+            gb[:, i] = jnp.zeros_like(gb[:, i])
+
+    pool(0)
+    pool(2)
+
+    def edge_taps(i, carry):
+        up_taps(2 * i)
         return carry
 
-    lax.fori_loop(0, 9, up_tap, 0)
+    lax.fori_loop(0, 2, edge_taps, 0)
     grad_two = norm_back(up[...], n2[...], s2[...])
     up[...] = grad_two
     g2[1] = grad_two.astype(BF).reshape(4, n, c1)
@@ -233,32 +239,28 @@
         copy.start()
 
     zero_pad = jnp.zeros((2, n, 3 * c1), BF)
-    for rr in range(3):
-        xc[rr, pl.ds(4, 2)] = zero_pad
+    xc[1, pl.ds(4, 2)] = zero_pad
     spread(grad_two.astype(BF).astype(F32), xc, 1, 0, True)
     acc[...] = jnp.zeros_like(acc)
 
-    def back_tap(a, b):
-        for e in range(3):
-            left = xc[2 - b, pl.ds(2 - a, 4), :, pl.ds(e * c1, c1)].reshape(rows, c1)
-            acc[...] += lax.dot_general(left, wm[a, b, e], NT, preferred_element_type=F32)
-
-    def own_tap(a, carry):
-        back_tap(a, 1)
-        return carry
-
-    lax.fori_loop(0, 3, own_tap, 0)
+    def back_taps(b):
+        for a in range(3):
+            for e in range(3):
+                left = xc[2 - b, pl.ds(2 - a, 2 + a), :, pl.ds(e * c1, c1)].reshape((2 + a) * n, c1)
+                acc[pl.ds(0, (2 + a) * n)] += lax.dot_general(left, wm[a, b, e], NT, preferred_element_type=F32)
+
+    back_taps(1)
     for copy in g_copies:
         copy.wait_recv()
     for rr, ok in ((0, low_ok), (2, high_ok)):
         halo = g2[rr].reshape(rows, c1).astype(F32)
         spread(jnp.where(ok, halo, 0.0), xc, rr, 0, True)
 
-    def halo_tap(i, carry):
-        back_tap(i // 2, (i % 2) * 2)
+    def halo_taps(i, carry):
+        back_taps(2 * i)
         return carry
 
-    lax.fori_loop(0, 6, halo_tap, 0)
+    lax.fori_loop(0, 2, halo_taps, 0)
     grad_one = up[...] + norm_back(acc[...], n1[...], s1[...])
     spread(grad_one.astype(BF).astype(F32), xc, 1, 0, True)
     total = jnp.zeros((n, 128), F32)

time: 50.2 us -> 46.7 us (0.930)
  Pallas kernels: 49.4 us -> 45.9 us
    pallas_call x1, Pallas kernels: 47.9 us -> 44.4 us  [shards(): pl.pallas_call(functools.partial(kernel, n), out_shape=(jax.ShapeDtypeStr...]
where the time goes in v3:
time: 46.7 us; the launch traced here: 46.6 us
  Pallas kernels  45.9 us (98%)
  between operations  0.64 us (1%)
    pallas_call x1, Pallas kernels, shards(): pl.pallas_call(functools.partial(kernel, n), out_shape=(jax.ShapeDtypeStr...  44.4 us
    pallas_call x1, Pallas kernels, shards(): pl.pallas_call(close_kernel, out_shape=(jax.ShapeDtypeStruct(decoded.shap...  1.55 us

profile of v3, /device:TPU:1, one launch (start us, length us, event | category | flops | bytes accessed | tf_op | source)
XLA Modules:
  0.0 46.6 jit_solution(13318005828781891358)
XLA Ops:
  0.6 44.4 %shard_map.68 = (bf16[2,2,96,128]{3,2,1,0:T(8,128)(2,1)}, f32[2,16,64]{2,1,0:T(8,128)}) custom-call(bf16[2,16,64]{2,1,0:T(8,128)(2,1)} %bitcast.13, bf16[2,2,96,128]{3,2,1,0:T(8,128)(2,1)} %bitcast.12, bf16[3,3,3,16,384]{4,3,2,1,0:T(8,128)(2,1)} %win_hbm.1, bf16[3,3,3,384,384]{4,3,2,1,0:T(8,128)(2,1)} %wm_hbm.1, bf16[3,3,3,192,384]{4,3,2,1,0:T(8,128)(2,1)} %bitcast.11), custom_call_target="tpu_custom_call" | custom-call | tf_op jit(solution)/shard_map/pallas_call | solution.py:337
  45.0 1.5 %shard_map.69 = (bf16[2,2,96,128]{3,2,1,0:T(8,128)(2,1)}, f32[2,16,64]{2,1,0:T(8,128)}) custom-call(bf16[2,2,96,128]{3,2,1,0:T(8,128)(2,1)} %get-tuple-element.6.dec_in, f32[2,16,64]{2,1,0:T(8,128)} %get-tuple-element.7.lg_in), custom_call_target="tpu_custom_call" | custom-call | tf_op jit(solution)/shard_map/pallas_call | solution.py:376

commit v4 on v3

--- a/solution.py
+++ b/solution.py
@@ -42,6 +42,10 @@
     for copy in copies[:1] + [own] + copies[1:]:
         copy.start()
 
+    @pl.when(s == 1)
+    def _():
+        gb[pl.ds(0, 2), pl.ds(1, 2)] = jnp.zeros((2, 2, 2, c2 // 2, 2 * n), BF)
+
     barrier = pltpu.get_barrier_semaphore()
 
     def greet(ps, to, pc):
@@ -74,7 +78,7 @@
         x = jnp.concatenate([lat_in[f].astype(F32), jnp.zeros((16, 128 - n), F32)], axis=1)
         stack = [pltpu.roll(x, (2 - r) % 128, axis=1) if r != 2 else x for r in range(5)]
         both = jnp.concatenate(stack + [jnp.zeros((48, 128), F32)], axis=0)
-        view[f] = both.T[:n].reshape(n, 1, 128)
+        view[:, f] = both.T[:n].reshape(n, 1, 128)
 
     pick_row = lax.broadcasted_iota(jnp.int32, (n, 2 * n), 0)
     pick_col = lax.broadcasted_iota(jnp.int32, (n, 2 * n), 1)
@@ -95,8 +99,7 @@
                 for t in range(2):
                     j = t + 2 - a
                     wz[j, e, pl.ds(b * 32 + t * 16, 16), :] = piece
-    for i in range(2):
-        lat[2 * s + i, l] = view[i, l]
+    lat[s, l] = view[l]
 
     pl.semaphore_wait(barrier, 2 * n + 1)
 
@@ -106,19 +109,30 @@
     x_copies = []
     for k, (ps, pc) in enumerate(peers):
         x_copies.append(remote(rew_hbm, gb.at[pl.ds(2 * s, 2), pl.ds(1, 2), c], xs_s.at[k], xs_r.at[k], (ps, l, pc)))
-        x_copies[-1].start()
+
+    @pl.when(s == 1)
+    def _():
+        x_copies[0].start()
+        x_copies[2].start()
+
+    x_copies[1].start()
 
     def send_lat(to):
-        remote(view.at[:, to], lat.at[pl.ds(2 * s, 2), l], la_s.at[0], la_r.at[0], (s, to, c)).start()
-        remote(view.at[:, to], lat.at[pl.ds(2 * s, 2), l], la_s.at[1], la_r.at[1], (1 - s, to, c)).start()
+        remote(view.at[to], lat.at[s, l], la_s.at[0], la_r.at[0], (s, to, c)).start()
+        remote(view.at[to], lat.at[s, l], la_s.at[1], la_r.at[1], (1 - s, to, c)).start()
 
     each_partner(send_lat)
-    other = remote(view.at[:, l], lat.at[pl.ds(2 * s, 2), l], la_s.at[1], la_r.at[1], (1 - s, l, c))
+    other = remote(view.at[l], lat.at[s, l], la_s.at[1], la_r.at[1], (1 - s, l, c))
     other.start()
 
     own.wait()
-    for copy in x_copies:
-        copy.wait_recv()
+
+    @pl.when(s == 0)
+    def _():
+        x_copies[0].wait_recv()
+        x_copies[2].wait_recv()
+
+    x_copies[1].wait_recv()
     r_copies = [
         remote(gb.at[:, 2], gb.at[:, 0], rs_s.at[0], rs_r.at[0], (s, nxt, c)),
         remote(gb.at[:, 1], gb.at[:, 3], rs_s.at[1], rs_r.at[1], (s, prv, c)),
@@ -126,11 +140,11 @@
     for copy in r_copies:
         copy.start()
 
-    wait_bytes(lat.at[pl.ds(0, 2), pl.ds(0, n - 1)], la_r.at[0])
-    wait_bytes(lat.at[pl.ds(0, 2)], la_r.at[1])
+    wait_bytes(lat.at[0, pl.ds(0, n - 1)], la_r.at[0])
+    wait_bytes(lat.at[0], la_r.at[1])
 
     for f in range(4):
-        x = lat[f].reshape(n, 128)
+        x = lat[f // 2, :, f % 2].reshape(n, 128)
         for e in range(3):
             moved = (shift_rows(x, 1 - e, row, n) if e != 1 else x).astype(BF)
             for a in range(3):
@@ -180,7 +194,8 @@
             acc[part] += jnp.dot(left, wm[a, b].reshape(3 * c1, c1), preferred_element_type=F32)
         return carry
 
-    lax.fori_loop(0, 3, mid_taps, 0)
+    for i in range(3):
+        mid_taps(i, 0)
     normed, inv, hidden = norm(acc[...])
     n2[...] = normed
     s2[...] = inv
@@ -227,7 +242,8 @@
         up_taps(2 * i)
         return carry
 
-    lax.fori_loop(0, 2, edge_taps, 0)
+    for i in range(2):
+        edge_taps(i, 0)
     grad_two = norm_back(up[...], n2[...], s2[...])
     up[...] = grad_two
     g2[1] = grad_two.astype(BF).reshape(4, n, c1)
@@ -260,7 +276,8 @@
         back_taps(2 * i)
         return carry
 
-    lax.fori_loop(0, 2, halo_taps, 0)
+    for i in range(2):
+        halo_taps(i, 0)
     grad_one = up[...] + norm_back(acc[...], n1[...], s1[...])
     spread(grad_one.astype(BF).astype(F32), xc, 1, 0, True)
     total = jnp.zeros((n, 128), F32)
@@ -314,10 +331,15 @@
     result = shift_rows(z, -1, row, n) + pltpu.roll(z, 128 - 32, axis=1) + pltpu.roll(shift_rows(z, 1, row, n), 128 - 64, axis=1)
     lg_out[...] = result.T[:32].reshape(2, 16, n)
 
-    wait_bytes(view.at[:, pl.ds(0, n - 1)], la_s.at[0])
+    wait_bytes(view.at[pl.ds(0, n - 1)], la_s.at[0])
     wait_bytes(view, la_s.at[1])
     wait_bytes(zs.at[pl.ds(0, n - 1)], zsem.at[0])
-    for copy in x_copies + r_copies + h_copies + g_copies:
+    @pl.when(s == 1)
+    def _():
+        x_copies[0].wait_send()
+        x_copies[2].wait_send()
+
+    for copy in x_copies[1:2] + r_copies + h_copies + g_copies:
         copy.wait_send()
 
 
@@ -351,8 +373,8 @@
             vm((3 * n, 2 * n), BF),
             vm((2, 2 * n, c2 // 2), F32),
             vm((4, 4, 2, c2 // 2, 2 * n), BF),
-            vm((2, n, 1, 128), F32),
-            vm((4, n, 1, 128), F32),
+            vm((n, 2, 1, 128), F32),
+            vm((2, n, 2, 1, 128), F32),
             vm((4, n, 1152), BF),
             vm((3, 6, n, 3 * c1), BF),
             vm((3, 6, n, c1), BF),

time: 46.7 us -> 45.5 us (0.974)
  Pallas kernels: 45.9 us -> 44.7 us
    pallas_call x1, Pallas kernels: 44.4 us -> 43.2 us  [shards(): pl.pallas_call(functools.partial(kernel, n), out_shape=(jax.ShapeDtypeStr...]
where the time goes in v4:
time: 45.5 us; the launch traced here: 45.4 us
  Pallas kernels  44.7 us (98%)
  between operations  0.64 us (1%)
    pallas_call x1, Pallas kernels, shards(): pl.pallas_call(functools.partial(kernel, n), out_shape=(jax.ShapeDtypeStr...  43.2 us
    pallas_call x1, Pallas kernels, shards(): pl.pallas_call(close_kernel, out_shape=(jax.ShapeDtypeStruct(decoded.shap...  1.55 us

profile of v4, /device:TPU:1, one launch (start us, length us, event | category | flops | bytes accessed | tf_op | source)
XLA Modules:
  0.0 45.4 jit_solution(10894315950119405806)
XLA Ops:
  0.6 43.2 %shard_map.68 = (bf16[2,2,96,128]{3,2,1,0:T(8,128)(2,1)}, f32[2,16,64]{2,1,0:T(8,128)}) custom-call(bf16[2,16,64]{2,1,0:T(8,128)(2,1)} %bitcast.13, bf16[2,2,96,128]{3,2,1,0:T(8,128)(2,1)} %bitcast.12, bf16[3,3,3,16,384]{4,3,2,1,0:T(8,128)(2,1)} %win_hbm.1, bf16[3,3,3,384,384]{4,3,2,1,0:T(8,128)(2,1)} %wm_hbm.1, bf16[3,3,3,192,384]{4,3,2,1,0:T(8,128)(2,1)} %bitcast.11), custom_call_target="tpu_custom_call" | custom-call | tf_op jit(solution)/shard_map/pallas_call | solution.py:359
  43.8 1.5 %shard_map.69 = (bf16[2,2,96,128]{3,2,1,0:T(8,128)(2,1)}, f32[2,16,64]{2,1,0:T(8,128)}) custom-call(bf16[2,2,96,128]{3,2,1,0:T(8,128)(2,1)} %get-tuple-element.6.dec_in, f32[2,16,64]{2,1,0:T(8,128)} %get-tuple-element.7.lg_in), custom_call_target="tpu_custom_call" | custom-call | tf_op jit(solution)/shard_map/pallas_call | solution.py:398

commit v5 on v4

--- a/solution.py
+++ b/solution.py
@@ -51,24 +51,24 @@
     def greet(ps, to, pc):
         pl.semaphore_signal(barrier, inc=1, device_id=(ps, to, pc), device_id_type=MESH)
 
-    chunk = 9 if (n - 1) % 9 == 0 else n - 1
-
     def each_partner(act):
-        def step(k, carry):
-            for i in range(chunk):
-                act(lax.rem(l + k * chunk + (1 + i), n))
+        act(lax.rem(l + n // 2, n))
+
+        def step(d, carry):
+            act(lax.rem(l + n // 2 - d, n))
+            act(lax.rem(l + n // 2 + d, n))
             return carry
 
-        lax.fori_loop(0, (n - 1) // chunk, step, 0)
+        lax.fori_loop(1, n // 2, step, 0)
 
     def greet_all(to):
         greet(s, to, c)
         greet(1 - s, to, c)
 
     peers = [(1 - s, c), (s, 1 - c), (1 - s, 1 - c)]
+    each_partner(greet_all)
     for ps, pc in peers:
         greet(ps, l, pc)
-    each_partner(greet_all)
 
     def remote(src, dst, ss, rs, dev):
         return pltpu.make_async_remote_copy(src_ref=src, dst_ref=dst, send_sem=ss, recv_sem=rs, device_id=dev, device_id_type=MESH)

time: 45.5 us -> 44.7 us (0.982)
  Pallas kernels: 44.7 us -> 43.9 us
    pallas_call x1, Pallas kernels: 43.2 us -> 42.3 us  [shards(): pl.pallas_call(functools.partial(kernel, n), out_shape=(jax.ShapeDtypeStr...]
where the time goes in v5:
time: 44.7 us; the launch traced here: 44.5 us
  Pallas kernels  43.9 us (98%)
  between operations  0.64 us (1%)
    pallas_call x1, Pallas kernels, shards(): pl.pallas_call(functools.partial(kernel, n), out_shape=(jax.ShapeDtypeStr...  42.3 us
    pallas_call x1, Pallas kernels, shards(): pl.pallas_call(close_kernel, out_shape=(jax.ShapeDtypeStruct(decoded.shap...  1.55 us

profile of v5, /device:TPU:1, one launch (start us, length us, event | category | flops | bytes accessed | tf_op | source)
XLA Modules:
  0.0 44.5 jit_solution(3791710521093281485)
XLA Ops:
  0.6 42.3 %shard_map.68 = (bf16[2,2,96,128]{3,2,1,0:T(8,128)(2,1)}, f32[2,16,64]{2,1,0:T(8,128)}) custom-call(bf16[2,16,64]{2,1,0:T(8,128)(2,1)} %bitcast.13, bf16[2,2,96,128]{3,2,1,0:T(8,128)(2,1)} %bitcast.12, bf16[3,3,3,16,384]{4,3,2,1,0:T(8,128)(2,1)} %win_hbm.1, bf16[3,3,3,384,384]{4,3,2,1,0:T(8,128)(2,1)} %wm_hbm.1, bf16[3,3,3,192,384]{4,3,2,1,0:T(8,128)(2,1)} %bitcast.11), custom_call_target="tpu_custom_call" | custom-call | tf_op jit(solution)/shard_map/pallas_call | solution.py:359
  43.0 1.5 %shard_map.69 = (bf16[2,2,96,128]{3,2,1,0:T(8,128)(2,1)}, f32[2,16,64]{2,1,0:T(8,128)}) custom-call(bf16[2,2,96,128]{3,2,1,0:T(8,128)(2,1)} %get-tuple-element.6.dec_in, f32[2,16,64]{2,1,0:T(8,128)} %get-tuple-element.7.lg_in), custom_call_target="tpu_custom_call" | custom-call | tf_op jit(solution)/shard_map/pallas_call | solution.py:398
